TPU v7x, 32 devices: a whole 2x2x4 slice. The times are simulated.
32 devices in a mesh: context: 8 (over z, y), tensor: 4 (over x, core).
Axes of the slice: x: 2, y: 2, z: 4, core: 2. Of those that a mesh axis runs over, the one named last changes fastest.
Arguments:
- tokens: bfloat16 [4096, 4096], P(('context', 'tensor')), may hold values from -6 to 6
- norm_gain: float32 [4096], replicated, may hold values from 0.5 to 1.5
- in_weight: bfloat16 [4096, 3, 2048], P(None, None, 'tensor'), may hold values from -0.09375 to 0.09375
- short_weight: float32 [3, 3, 2048], P(None, None, 'tensor'), may hold values from -3 to 3
- long_filter: float32 [4096, 2048], P('context', 'tensor'), may hold values from -0.09375 to 0.09375
- skip_gain: float32 [2048], P('tensor'), may hold values from -4 to 4
Outputs:
- block_out: bfloat16 [4096, 2048], P('context', 'tensor')
All inputs are finite; a program needn't handle non-finite values.
Results may differ from a plain program's by a relative error of at most 0.0065.
Values may be sent and summed in bfloat16 or wider, within the bound.
No kernel may reach another device: no remote copies, remote signals or barrier semaphores. Data moves between devices by JAX's collectives and lax.ppermute only.
A program may use at most 128 MiB of HBM per device.

v0:
```python
import math
import jax
import jax.numpy as jnp
from jax import lax
from jax.sharding import PartitionSpec as P

eps = 1e-06


def shifted(x, axis, by):
    peers = lax.axis_size(axis)
    pairs = [(i, i + by) for i in range(peers) if 0 <= i + by < peers]
    return lax.ppermute(x, axis, pairs)


def along_rows(table, block):
    return jnp.einsum("kj,tjc->tkc", table, block, precision=lax.Precision.HIGHEST)


def transposed(stacked, forward):
    dev_count = lax.axis_size("context")
    planes, turn_count, length, channels = stacked.shape
    ranks = jnp.arange(dev_count, dtype=jnp.int32)
    phase_angle = (ranks[:, None] * ranks[None, :] % dev_count).astype(jnp.float32) * (
        2.0 * math.pi / dev_count
    )
    table_re = jnp.cos(phase_angle)
    if forward:
        table_im = -jnp.sin(phase_angle)
    else:
        table_im = jnp.sin(phase_angle)

    def combine_rows(received):
        rows_re = jnp.einsum(
            "fp,tpjc->tfjc", table_re, received[0], precision=lax.Precision.HIGHEST
        ) - jnp.einsum("fp,tpjc->tfjc", table_im, received[1], precision=lax.Precision.HIGHEST)
        rows_im = jnp.einsum(
            "fp,tpjc->tfjc", table_re, received[1], precision=lax.Precision.HIGHEST
        ) + jnp.einsum("fp,tpjc->tfjc", table_im, received[0], precision=lax.Precision.HIGHEST)
        return jnp.stack([rows_re, rows_im])

    sectioned = stacked.reshape(planes, turn_count, 1, length, channels)
    if forward:
        result_grid = lax.all_to_all(
            combine_rows(
                lax.all_to_all(sectioned, "context", split_axis=3, concat_axis=2, tiled=True)
            ),
            "context",
            split_axis=2,
            concat_axis=3,
            tiled=True,
        )
    else:
        result_grid = lax.all_to_all(
            combine_rows(
                lax.all_to_all(sectioned, "context", split_axis=3, concat_axis=2, tiled=True)
            ),
            "context",
            split_axis=2,
            concat_axis=3,
            tiled=True,
        )
    return result_grid.reshape(planes, turn_count, length, channels)


def local(tokens, norm_gain, in_weight, short_weight, long_filter, skip_gain):
    width = tokens.shape[1]
    channels = in_weight.shape[2]
    tap_count = short_weight.shape[0]
    flat_weight = in_weight.reshape(width, 3 * channels)
    values = lax.all_gather(tokens, "tensor", axis=0, tiled=True).astype(jnp.float32)
    inv_rms = lax.rsqrt(jnp.mean(values * values, axis=1, keepdims=True) + eps)
    normed = (values * inv_rms * norm_gain).astype(jnp.bfloat16)
    projected = jnp.dot(normed, flat_weight, preferred_element_type=jnp.float32)
    length = projected.shape[0]
    before = shifted(projected[length - (tap_count - 1) :], "context", 1)
    padded = jnp.concatenate([before, projected], axis=0)
    tap_rows = short_weight.reshape(tap_count, 3 * channels)
    mixed_rows = jnp.zeros_like(projected)
    for tap_index in range(tap_count):
        offset = tap_count - 1 - tap_index
        mixed_rows = mixed_rows + tap_rows[tap_index] * padded[offset : offset + length]
    query_part = mixed_rows[:, :channels]
    key_part = mixed_rows[:, channels : 2 * channels]
    value_part = mixed_rows[:, 2 * channels :]
    gated = key_part * value_part
    dev_count = lax.axis_size("context")
    device = lax.axis_index("context")
    total_points = 2 * dev_count * length
    half_turn = device.astype(jnp.float32) * (math.pi / dev_count)
    source = jnp.concatenate([gated, long_filter], axis=1)
    zero_plane = jnp.zeros_like(source)
    shifted_re = source * jnp.cos(half_turn)
    shifted_im = -source * jnp.sin(half_turn)
    stacked = jnp.stack([jnp.stack([source, shifted_re]), jnp.stack([zero_plane, shifted_im])])
    stacked = transposed(stacked, True)
    turn_ids = jnp.arange(2, dtype=jnp.int32)
    coarse = 2 * device + turn_ids
    positions = jnp.arange(length, dtype=jnp.int32)
    twist_phase = (positions[None, :] * coarse[:, None] % total_points).astype(jnp.float32) * (
        2.0 * math.pi / total_points
    )
    twist_re = jnp.cos(twist_phase)[:, :, None]
    twist_im = -jnp.sin(twist_phase)[:, :, None]
    turned_re = stacked[0] * twist_re - stacked[1] * twist_im
    turned_im = stacked[0] * twist_im + stacked[1] * twist_re
    table_phase = (positions[:, None] * positions[None, :] % length).astype(jnp.float32) * (
        2.0 * math.pi / length
    )
    cos_table = jnp.cos(table_phase)
    sin_table = jnp.sin(table_phase)
    spec_re = along_rows(cos_table, turned_re) + along_rows(sin_table, turned_im)
    spec_im = along_rows(cos_table, turned_im) - along_rows(sin_table, turned_re)
    signal_re = spec_re[:, :, :channels]
    signal_im = spec_im[:, :, :channels]
    filt_re = spec_re[:, :, channels:]
    filt_im = spec_im[:, :, channels:]
    prod_re = signal_re * filt_re - signal_im * filt_im
    prod_im = signal_re * filt_im + signal_im * filt_re
    back_re = along_rows(cos_table, prod_re) - along_rows(sin_table, prod_im)
    back_im = along_rows(sin_table, prod_re) + along_rows(cos_table, prod_im)
    untw_re = back_re * twist_re + back_im * twist_im
    untw_im = back_im * twist_re - back_re * twist_im
    stacked = jnp.stack([untw_re, untw_im])
    stacked = transposed(stacked, False)
    conv = (
        stacked[0, 0] + stacked[0, 1] * jnp.cos(half_turn) - stacked[1, 1] * jnp.sin(half_turn)
    ) / total_points
    block_out = query_part * (conv + skip_gain * gated)
    return block_out.astype(jnp.bfloat16)


def solution(mesh):
    return jax.shard_map(
        local,
        mesh=mesh,
        in_specs=(
            P(("context", "tensor"), None),
            P(),
            P(None, None, "tensor"),
            P(None, None, "tensor"),
            P("context", "tensor"),
            P("tensor"),
        ),
        out_specs=P("context", "tensor"),
        check_vma=False,
    )
```

profile of v0, /device:TPU:0, one launch (start us, length us, event | category | flops | bytes accessed | tf_op | source)
XLA Modules:
  0.0 858.5 jit_solution(13042086948463147038)
XLA Ops:
  7.3 17.1 %copy.52 = bf16[4096,3,512]{0,2,1:T(8,128)(2,1)} copy(bf16[4096,3,512]{2,0,1:T(8,128)(2,1)} %param.8) | data formatting | bytes 25165824 | tf_op args[2]
  24.3 21.8 %all-gather.2.cloned.1.call-done = bf16[512,4096]{1,0:T(8,128)(2,1)} async-done(((bf16[128,4096]{1,0:T(8,128)(2,1)}), bf16[512,4096]{1,0:T(8,128)(2,1)}) %all-gather.2.cloned.1.call-update) | async-done | bytes 4194320 | tf_op jit(solution)/shard_map/all_gather | solution.py:71
  46.1 3.2 fusion
  49.6 9.4 %fusion.3 = f32[512,1536]{1,0:T(8,128)S(1)} fusion(bf16[4096,1536]{0,1:T(8,128)(2,1)} %bitcast.124, bf16[512,4096]{1,0:T(8,128)(2,1)S(1)} %copy-done.1, f32[4096]{0:T(1024)S(1)} %copy-done.6, f32[512]{0:T(512)S(1)} %add_rsqrt_fusion), kind=kOutput, calls=%fused_computation.7 | convolution fusion | flops 6450839552 | bytes 19941376 | tf_op jit(solution)/shard_map/dot_general | solution.py:74
  59.0 3.4 collective-permute-start
  63.8 4.9 fusion.18
  73.2 7.4 copy.53
  80.6 188.8 %all_to_all.16 = f32[2,2,1,512,1024]{4,1,0,2,3:T(2,128)} all-to-all(f32[2,2,1,512,1024]{4,1,0,2,3:T(2,128)S(1)} %copy.53), channel_id=1, replica_groups=mesh['context'=8,'tensor'=4] {'context'}, dimensions={3} | all-to-all | bytes 16777216 | tf_op jit(solution)/shard_map/all_to_all | solution.py:46
  269.4 9.6 %fusion.167 = (f32[1,2,1,512,1024]{4,1,0,2,3:T(2,128)}, f32[1,2,1,512,1024]{4,1,0,2,3:T(2,128)}) fusion(f32[2,2,1,512,1024]{4,1,0,2,3:T(2,128)} %all_to_all.16), kind=kLoop, calls=%fused_computation.185 | loop fusion | bytes 16777216 | tf_op jit(solution)/shard_map/slice | solution.py:35
  279.0 3.5 copy.84
  282.5 7.8 fusion.9
  290.3 8.1 fusion.7
  299.8 8.1 subtract_bitcast_fusion.1
  307.9 8.0 add_bitcast_fusion.1
  317.6 8.5 copy.60
  326.1 5.0 all-to-all-start.1
  331.2 181.8 %all-to-all-done.1 = f32[2,2,8,64,1024]{4,3,1,0,2:T(8,128)} async-done(((f32[2,2,8,64,1024]{4,3,1,0,2:T(8,128)}), f32[2,2,8,64,1024]{4,3,1,0,2:T(8,128)}, u32[]{:S(2)}, u32[]{:S(2)}) %all-to-all-start.1) | async-done | bytes 8388640 | tf_op jit(solution)/shard_map/all_to_all | solution.py:44
  513.0 4.3 fusion.166
  518.3 18.1 %fusion.37 = f32[2,1024,512]{2,1,0:T(8,128)S(1)} fusion(f32[2,512,1024]{2,1,0:T(8,128)S(1)} %bitcast.111, f32[2,512,1024]{2,1,0:T(8,128)S(1)} %bitcast.107, f32[2,512]{1,0:T(2,128)S(1)} %get-tuple-element.21, f32[2,512]{1,0:T(2,128)S(1)} %get-tuple-element.20), kind=kOutput, calls=%fused_computation.59 | convolution fusion | flops 6449266688 | bytes 12591104 | tf_op jit(solution)/shard_map/kj,tjc->tkc/dot_general | solution.py:17
  536.4 18.5 %fusion.38 = f32[2,1024,512]{2,1,0:T(8,128)S(1)} fusion(f32[2,512,1024]{2,1,0:T(8,128)S(1)} %bitcast.112, f32[2,512,1024]{2,1,0:T(8,128)S(1)} %bitcast.108, f32[2,512]{1,0:T(2,128)S(1)} %get-tuple-element.21, f32[2,512]{1,0:T(2,128)S(1)} %get-tuple-element.20), kind=kOutput, calls=%fused_computation.60 | convolution fusion | flops 6449266688 | bytes 12591104 | tf_op jit(solution)/shard_map/kj,tjc->tkc/dot_general | solution.py:17
  554.9 18.2 %add_bitcast_fusion = f32[2,512,1024]{1,2,0:T(8,128)S(1)} fusion(f32[2,1024,512]{2,1,0:T(8,128)S(1)} %fusion.37, f32[2,512,1024]{2,1,0:T(8,128)S(1)} %bitcast.113, f32[2,512,1024]{2,1,0:T(8,128)S(1)} %bitcast.109, f32[2,512]{1,0:T(2,128)S(1)} %get-tuple-element.21, f32[2,512]{1,0:T(2,128)S(1)} %get-tuple-element.20), kind=kOutput, calls=%fused_computation.12 | convolution fusion | flops 6450315264 | bytes 16785408 | tf_op jit(solution)/shard_map/kj,tjc->tkc/dot_general | solution.py:17
  573.1 18.6 %subtract_bitcast_fusion = f32[2,512,1024]{1,2,0:T(8,128)S(1)} fusion(f32[2,1024,512]{2,1,0:T(8,128)S(1)} %fusion.38, f32[2,512,1024]{2,1,0:T(8,128)S(1)} %bitcast.114, f32[2,512,1024]{2,1,0:T(8,128)S(1)} %bitcast.110, f32[2,512]{1,0:T(2,128)S(1)} %get-tuple-element.21, f32[2,512]{1,0:T(2,128)S(1)} %get-tuple-element.20), kind=kOutput, calls=%fused_computation.11 | convolution fusion | flops 6450315264 | bytes 16785408 | tf_op jit(solution)/shard_map/kj,tjc->tkc/dot_general | solution.py:17
  593.1 8.4 fusion.49
  601.5 8.4 fusion.55
  609.9 8.6 %convolution_add_fusion = f32[2,512,512]{2,1,0:T(8,128)S(1)} fusion(f32[2,512,512]{2,1,0:T(8,128)S(1)} %fusion.49, f32[2,512,512]{1,2,0:T(8,128)S(1)} %get-tuple-element.5), kind=kOutput, calls=%fused_computation.54 | convolution fusion | flops 3225419776 | bytes 6291456 | tf_op jit(solution)/shard_map/kj,tjc->tkc/dot_general | solution.py:17
  618.6 8.7 %add_bitcast_fusion.3 = (f32[1,2,512,512]{2,3,1,0:T(8,128)S(1)}, f32[1,2,512,512]{2,3,1,0:T(8,128)S(1)}) fusion(f32[2,512,512]{2,1,0:T(8,128)S(1)} %convolution_add_fusion, f32[2,512]{1,0:T(2,128)S(1)} %get-tuple-element.21, f32[2,512]{1,0:T(2,128)S(1)} %get-tuple-element.20, f32[2,512,512]{2,1,0:T(8,128)S(1)} %fusion.55, ...), kind=kOutput, calls=%fused_computation.41 | convolution fusion | flops 3228565504 | bytes 10493952 | tf_op jit(solution)/shard_map/kj,tjc->tkc/dot_general | solution.py:17
  629.7 7.3 copy.67
  637.0 96.9 %all_to_all.17 = f32[2,2,1,512,512]{4,1,0,2,3:T(2,128)S(1)} all-to-all(f32[2,2,1,512,512]{4,1,0,2,3:T(2,128)} %copy.67), channel_id=1, replica_groups=mesh['context'=8,'tensor'=4] {'context'}, dimensions={3} | all-to-all | bytes 8388608 | tf_op jit(solution)/shard_map/all_to_all | solution.py:56
  739.0 3.2 fusion.24
  742.6 3.6 subtract_bitcast_fusion.2
  746.2 3.4 add_bitcast_fusion.2
  752.5 96.5 %all_to_all.18 = f32[2,2,8,64,512]{4,3,1,0,2:T(8,128)S(1)} all-to-all(f32[2,2,8,64,512]{4,3,1,0,2:T(8,128)S(1)} %copy.74), channel_id=1, replica_groups=mesh['context'=8,'tensor'=4] {'context'}, dimensions={2} | all-to-all | bytes 8388608 | tf_op jit(solution)/shard_map/all_to_all | solution.py:54
  (45 shorter events, 25.0 us)
Async XLA Ops:
  6.5 39.6 %all-gather.2.cloned.1.call-start = ((), (), s32[]{:S(2)}) async-start(), calls=%async_computation.4 | async-start | bytes 5242880 | tf_op jit(solution)/shard_map/all_gather | solution.py:71
  7.3 42.1 %copy-start.6 = (f32[4096]{0:T(1024)S(1)}, f32[4096]{0:T(1024)}, u32[]{:S(2)}) copy-start(f32[4096]{0:T(1024)} %param.7) | copy-start | bytes 49156
  46.1 3.4 copy-start.1
  49.6 12.9 %copy-start.4 = (f32[3,3,512]{2,1,0:T(4,128)S(1)}, f32[3,3,512]{2,1,0:T(4,128)}, u32[]{:S(2)}) copy-start(f32[3,3,512]{2,1,0:T(4,128)} %param.9) | copy-start | bytes 55300
  59.0 3.6 copy-start.3
  59.0 4.8 collective-permute-start
  68.7 1.2 copy-start.2
  290.3 8.2 copy-start
  326.1 186.9 %all-to-all-start.1 = ((f32[2,2,8,64,1024]{4,3,1,0,2:T(8,128)}), f32[2,2,8,64,1024]{4,3,1,0,2:T(8,128)}, u32[]{:S(2)}, u32[]{:S(2)}) async-start(f32[2,2,8,64,1024]{4,3,1,0,2:T(8,128)} %copy.60), calls=%async_computation.1 | async-start | bytes 16777216 | tf_op jit(solution)/shard_map/all_to_all | solution.py:44
  849.0 0.7 copy-start.5
Sparse Core Ops, SparseCore 0:
  8.9 37.1 all-gather.1
where the time goes:
time: 865 us; the launch traced here: 859 us
  blocking collectives  382 us (44%)
  waiting for transfers between devices  205 us (24%)
  matrix products  162 us (19%)
  local copies, waits for them, and re-layouts  66.5 us (8%)
  other arithmetic  19.3 us (2%)
  between operations  14.4 us (2%)
    all_to_all x2, blocking collectives, transposed(): lax.all_to_all(sectioned, 'context', split_axis=3, concat_axis=2, tiled=T...  286 us
    all_to_all x1, waiting for transfers between devices, transposed(): lax.all_to_all(combine_rows(lax.all_to_all(sectioned, 'context', split_ax...  182 us
    dot_general x8, matrix products, along_rows(): jnp.einsum('kj,tjc->tkc', table, block, precision=lax.Precision.HIGHEST)  108 us
    all_to_all x1, blocking collectives, transposed(): lax.all_to_all(combine_rows(lax.all_to_all(sectioned, 'context', split_ax...  96.5 us
    unnamed x21, local copies, waits for them, and re-layouts  24.8 us
    all_gather x1, waiting for transfers between devices, local(): lax.all_gather(tokens, 'tensor', axis=0, tiled=True).astype(jnp.float32)  21.8 us
  transfers between devices with their start and end apart: 3, of which 3 were waited for; matrix products, arithmetic and copies ran while one was open for 2% of the time, Pallas kernels for 0%

commit v1 on v0

--- a/solution.py
+++ b/solution.py
@@ -5,6 +5,33 @@
 from jax.sharding import PartitionSpec as P
 
 eps = 1e-06
+
+
+def counts_define(message):
+    clean = jax.lax.axis_size("tensor")
+    val2 = jax.lax.axis_index("tensor")
+    base_arr, next_value, current_block = (clean, val2, message.shape[0])
+    grid = list(map(lambda ix: (ix, (ix + 1) % base_arr), range(base_arr)))
+    gallery = list(map(lambda ix: (ix, (ix - 1) % base_arr), range(base_arr)))
+    all_rows = jnp.zeros(
+        (*message.shape[:0], base_arr * current_block, *message.shape[1:]), message.dtype
+    )
+    all_rows = lax.dynamic_update_slice_in_dim(
+        all_rows, message, next_value * current_block, axis=0
+    )
+    state_now = base_arr // 2
+    block_last = tile_out = message
+    for jj in range(1, state_now + 1):
+        block_last = jax.lax.ppermute(block_last, "tensor", grid)
+        all_rows = lax.dynamic_update_slice_in_dim(
+            all_rows, block_last, (next_value - jj) % base_arr * current_block, axis=0
+        )
+        if jj < base_arr - state_now:
+            tile_out = jax.lax.ppermute(tile_out, "tensor", gallery)
+            all_rows = lax.dynamic_update_slice_in_dim(
+                all_rows, tile_out, (next_value + jj) % base_arr * current_block, axis=0
+            )
+    return all_rows
 
 
 def shifted(x, axis, by):
@@ -68,7 +95,7 @@
     channels = in_weight.shape[2]
     tap_count = short_weight.shape[0]
     flat_weight = in_weight.reshape(width, 3 * channels)
-    values = lax.all_gather(tokens, "tensor", axis=0, tiled=True).astype(jnp.float32)
+    values = counts_define(tokens).astype(jnp.float32)
     inv_rms = lax.rsqrt(jnp.mean(values * values, axis=1, keepdims=True) + eps)
     normed = (values * inv_rms * norm_gain).astype(jnp.bfloat16)
     projected = jnp.dot(normed, flat_weight, preferred_element_type=jnp.float32)

time: 865 us -> 870 us (level)
  between operations: 14.4 us -> 0.99 us
  local copies, waits for them, and re-layouts: 66.5 us -> 75.8 us
    all_gather x1 -> x0, waiting for transfers between devices: 21.8 us -> none  [local(): lax.all_gather(tokens, 'tensor', axis=0, tiled=True).astype(jnp.float32)]
    ppermute x0 -> x3, waiting for transfers between devices: none -> 21.4 us  [the longest x2 21.4 us: counts_define(): block_last = jax.lax.ppermute(block_last, 'tensor', grid)]
  transfers between devices with their start and end apart: 3 -> 5, of which waited for: 3 -> 3; matrix products, arithmetic and copies ran while one was open for 2% -> 3% of each run, Pallas kernels for 0% -> 0%
where the time goes in v1:
time: 870 us; the launch traced here: 863 us
  blocking collectives  385 us (44%)
  waiting for transfers between devices  206 us (24%)
  matrix products  164 us (19%)
  local copies, waits for them, and re-layouts  75.8 us (9%)
  other arithmetic  19.1 us (2%)
  starting transfers between devices  12.6 us (1%)
    all_to_all x2, blocking collectives, transposed(): lax.all_to_all(sectioned, 'context', split_axis=3, concat_axis=2, tiled=T...  288 us
    all_to_all x1, waiting for transfers between devices, transposed(): lax.all_to_all(combine_rows(lax.all_to_all(sectioned, 'context', split_ax...  183 us
    dot_general x8, matrix products, along_rows(): jnp.einsum('kj,tjc->tkc', table, block, precision=lax.Precision.HIGHEST)  108 us
    all_to_all x1, blocking collectives, transposed(): lax.all_to_all(combine_rows(lax.all_to_all(sectioned, 'context', split_ax...  96.5 us
    unnamed x21, local copies, waits for them, and re-layouts  26.1 us
    ppermute x2, waiting for transfers between devices, counts_define(): block_last = jax.lax.ppermute(block_last, 'tensor', grid)  21.4 us
  transfers between devices with their start and end apart: 5, of which 3 were waited for; matrix products, arithmetic and copies ran while one was open for 3% of the time, Pallas kernels for 0%

profile of v1, /device:TPU:0, one launch (start us, length us, event | category | flops | bytes accessed | tf_op | source)
XLA Modules:
  0.0 862.8 jit_solution(14150730340586872842)
XLA Ops:
  2.4 21.4 %collective-permute-done = bf16[128,4096]{1,0:T(8,128)(2,1)S(1)} collective-permute-done((bf16[128,4096]{1,0:T(8,128)(2,1)}, bf16[128,4096]{1,0:T(8,128)(2,1)S(1)}, u32[]{:S(2)}, u32[]{:S(2)}) %collective-permute-start) | collective-permute-done | bytes 1048608 | tf_op jit(solution)/shard_map/ppermute | solution.py:25
  29.8 17.0 %copy.52 = bf16[4096,3,512]{0,2,1:T(8,128)(2,1)} copy(bf16[4096,3,512]{2,0,1:T(8,128)(2,1)} %param.8) | data formatting | bytes 25165824 | tf_op args[2]
  51.2 3.1 fusion
  54.3 10.7 %fusion.3 = f32[512,1536]{1,0:T(8,128)S(1)} fusion(bf16[4096,1536]{0,1:T(8,128)(2,1)} %bitcast.124, bf16[512,4096]{1,0:T(8,128)(2,1)} %constant_dynamic-update-slice_fusion, f32[4096]{0:T(1024)S(1)} %copy-done.6, f32[512]{0:T(512)S(1)} %add_rsqrt_fusion), kind=kOutput, calls=%fused_computation.7 | convolution fusion | flops 6450839552 | bytes 19941376 | tf_op jit(solution)/shard_map/dot_general | solution.py:101
  70.7 4.9 fusion.18
  80.0 7.4 copy.53
  87.4 191.4 %all_to_all.16 = f32[2,2,1,512,1024]{4,1,0,2,3:T(2,128)} all-to-all(f32[2,2,1,512,1024]{4,1,0,2,3:T(2,128)S(1)} %copy.53), channel_id=1, replica_groups=mesh['context'=8,'tensor'=4] {'context'}, dimensions={3} | all-to-all | bytes 16777216 | tf_op jit(solution)/shard_map/all_to_all | solution.py:73
  278.8 9.6 %fusion.167 = (f32[1,2,1,512,1024]{4,1,0,2,3:T(2,128)}, f32[1,2,1,512,1024]{4,1,0,2,3:T(2,128)}) fusion(f32[2,2,1,512,1024]{4,1,0,2,3:T(2,128)} %all_to_all.16), kind=kLoop, calls=%fused_computation.189 | loop fusion | bytes 16777216 | tf_op jit(solution)/shard_map/slice | solution.py:62
  288.4 3.5 copy.84
  291.9 7.8 fusion.9
  299.7 8.1 fusion.7
  309.2 8.1 subtract_bitcast_fusion.1
  317.4 8.0 add_bitcast_fusion.1
  327.0 8.5 copy.60
  335.5 5.0 all-to-all-start.1
  340.6 183.4 %all-to-all-done.1 = f32[2,2,8,64,1024]{4,3,1,0,2:T(8,128)} async-done(((f32[2,2,8,64,1024]{4,3,1,0,2:T(8,128)}), f32[2,2,8,64,1024]{4,3,1,0,2:T(8,128)}, u32[]{:S(2)}, u32[]{:S(2)}) %all-to-all-start.1) | async-done | bytes 8388640 | tf_op jit(solution)/shard_map/all_to_all | solution.py:71
  524.0 4.3 fusion.166
  529.4 18.1 %fusion.37 = f32[2,1024,512]{2,1,0:T(8,128)S(1)} fusion(f32[2,512,1024]{2,1,0:T(8,128)S(1)} %bitcast.111, f32[2,512,1024]{2,1,0:T(8,128)S(1)} %bitcast.107, f32[2,512]{1,0:T(2,128)S(1)} %get-tuple-element.21, f32[2,512]{1,0:T(2,128)S(1)} %get-tuple-element.20), kind=kOutput, calls=%fused_computation.59 | convolution fusion | flops 6449266688 | bytes 12591104 | tf_op jit(solution)/shard_map/kj,tjc->tkc/dot_general | solution.py:44
  547.5 18.5 %fusion.38 = f32[2,1024,512]{2,1,0:T(8,128)S(1)} fusion(f32[2,512,1024]{2,1,0:T(8,128)S(1)} %bitcast.112, f32[2,512,1024]{2,1,0:T(8,128)S(1)} %bitcast.108, f32[2,512]{1,0:T(2,128)S(1)} %get-tuple-element.21, f32[2,512]{1,0:T(2,128)S(1)} %get-tuple-element.20), kind=kOutput, calls=%fused_computation.60 | convolution fusion | flops 6449266688 | bytes 12591104 | tf_op jit(solution)/shard_map/kj,tjc->tkc/dot_general | solution.py:44
  566.0 18.2 %add_bitcast_fusion = f32[2,512,1024]{1,2,0:T(8,128)S(1)} fusion(f32[2,1024,512]{2,1,0:T(8,128)S(1)} %fusion.37, f32[2,512,1024]{2,1,0:T(8,128)S(1)} %bitcast.113, f32[2,512,1024]{2,1,0:T(8,128)S(1)} %bitcast.109, f32[2,512]{1,0:T(2,128)S(1)} %get-tuple-element.21, f32[2,512]{1,0:T(2,128)S(1)} %get-tuple-element.20), kind=kOutput, calls=%fused_computation.12 | convolution fusion | flops 6450315264 | bytes 16785408 | tf_op jit(solution)/shard_map/kj,tjc->tkc/dot_general | solution.py:44
  584.2 18.6 %subtract_bitcast_fusion = f32[2,512,1024]{1,2,0:T(8,128)S(1)} fusion(f32[2,1024,512]{2,1,0:T(8,128)S(1)} %fusion.38, f32[2,512,1024]{2,1,0:T(8,128)S(1)} %bitcast.114, f32[2,512,1024]{2,1,0:T(8,128)S(1)} %bitcast.110, f32[2,512]{1,0:T(2,128)S(1)} %get-tuple-element.21, f32[2,512]{1,0:T(2,128)S(1)} %get-tuple-element.20), kind=kOutput, calls=%fused_computation.11 | convolution fusion | flops 6450315264 | bytes 16785408 | tf_op jit(solution)/shard_map/kj,tjc->tkc/dot_general | solution.py:44
  604.1 8.4 fusion.49
  612.6 8.4 fusion.55
  621.0 8.6 convolution_add_fusion
  629.6 8.7 %add_bitcast_fusion.3 = (f32[1,2,512,512]{2,3,1,0:T(8,128)S(1)}, f32[1,2,512,512]{2,3,1,0:T(8,128)S(1)}) fusion(f32[2,512,512]{2,1,0:T(8,128)S(1)} %convolution_add_fusion, f32[2,512]{1,0:T(2,128)S(1)} %get-tuple-element.21, f32[2,512]{1,0:T(2,128)S(1)} %get-tuple-element.20, f32[2,512,512]{2,1,0:T(8,128)S(1)} %fusion.55, ...), kind=kOutput, calls=%fused_computation.41 | convolution fusion | flops 3228565504 | bytes 10493952 | tf_op jit(solution)/shard_map/kj,tjc->tkc/dot_general | solution.py:44
  640.7 7.3 copy.67
  648.0 96.9 %all_to_all.17 = f32[2,2,1,512,512]{4,1,0,2,3:T(2,128)S(1)} all-to-all(f32[2,2,1,512,512]{4,1,0,2,3:T(2,128)} %copy.67), channel_id=1, replica_groups=mesh['context'=8,'tensor'=4] {'context'}, dimensions={3} | all-to-all | bytes 8388608 | tf_op jit(solution)/shard_map/all_to_all | solution.py:83
  746.8 3.2 fusion.26
  750.0 3.2 fusion.24
  753.6 3.6 subtract_bitcast_fusion.2
  757.3 3.4 add_bitcast_fusion.2
  763.5 96.5 %all_to_all.18 = f32[2,2,8,64,512]{4,3,1,0,2:T(8,128)S(1)} all-to-all(f32[2,2,8,64,512]{4,3,1,0,2:T(8,128)S(1)} %copy.74), channel_id=1, replica_groups=mesh['context'=8,'tensor'=4] {'context'}, dimensions={2} | all-to-all | bytes 8388608 | tf_op jit(solution)/shard_map/all_to_all | solution.py:81
  (53 shorter events, 38.0 us)
Async XLA Ops:
  0.0 28.7 %copy-start.3 = (bf16[128,4096]{1,0:T(8,128)(2,1)S(1)}, bf16[128,4096]{1,0:T(8,128)(2,1)}, u32[]{:S(2)}) copy-start(bf16[128,4096]{1,0:T(8,128)(2,1)} %param.6) | copy-start | bytes 3145732
  0.0 23.8 %collective-permute-start = (bf16[128,4096]{1,0:T(8,128)(2,1)}, bf16[128,4096]{1,0:T(8,128)(2,1)S(1)}, u32[]{:S(2)}, u32[]{:S(2)}) collective-permute-start(bf16[128,4096]{1,0:T(8,128)(2,1)} %param.6), channel_id=1, source_target_pairs={{0,1},{1,2},{2,3},{3,0},{4,5},{5,6},{6,7},{7,4},{8,9},{9,10},{10,1... | collective-permute-start | bytes 3145736 | tf_op jit(solution)/shard_map/ppermute | solution.py:25
  0.5 47.4 %collective-permute-start.1 = (bf16[128,4096]{1,0:T(8,128)(2,1)}, bf16[128,4096]{1,0:T(8,128)(2,1)S(1)}, u32[]{:S(2)}, u32[]{:S(2)}) collective-permute-start(bf16[128,4096]{1,0:T(8,128)(2,1)} %param.6), channel_id=1, source_target_pairs={{0,3},{1,0},{2,1},{3,2},{4,7},{5,4},{6,5},{7,6},{8,11},{9,8},{10,9... | collective-permute-start | bytes 3145736 | tf_op jit(solution)/shard_map/ppermute | solution.py:30
  23.8 25.1 %collective-permute-start.2 = (bf16[128,4096]{1,0:T(8,128)(2,1)S(1)}, bf16[128,4096]{1,0:T(8,128)(2,1)}, u32[]{:S(2)}, u32[]{:S(2)}) collective-permute-start(bf16[128,4096]{1,0:T(8,128)(2,1)S(1)} %collective-permute-done), channel_id=1, source_target_pairs={{0,1},{1,2},{2,3},{3,0},{4,5},{5,6},{6,7},{7,4},{8,9},{9,10},{10,1... | collective-permute-start | bytes 3145736 | tf_op jit(solution)/shard_map/ppermute | solution.py:25
  47.8 6.4 copy-start.6
  54.3 15.0 %copy-start.4 = (f32[3,3,512]{2,1,0:T(4,128)S(1)}, f32[3,3,512]{2,1,0:T(4,128)}, u32[]{:S(2)}) copy-start(f32[3,3,512]{2,1,0:T(4,128)} %param.9) | copy-start | bytes 55300
  64.9 1.6 copy-start.2
  66.6 4.1 collective-permute-start.3
  75.6 1.2 copy-start.1
  299.7 8.2 copy-start
  335.5 188.5 %all-to-all-start.1 = ((f32[2,2,8,64,1024]{4,3,1,0,2:T(8,128)}), f32[2,2,8,64,1024]{4,3,1,0,2:T(8,128)}, u32[]{:S(2)}, u32[]{:S(2)}) async-start(f32[2,2,8,64,1024]{4,3,1,0,2:T(8,128)} %copy.60), calls=%async_computation.1 | async-start | bytes 16777216 | tf_op jit(solution)/shard_map/all_to_all | solution.py:71
  860.0 0.7 copy-start.5
